TPU v7x, 32 devices: a whole 2x2x4 slice. The times are simulated.
32 devices in a mesh: prow: 16 (over z, x, core), pcol: 2 (over y).
Axes of the slice: x: 2, y: 2, z: 4, core: 2. Of those that a mesh axis runs over, the one named last changes fastest.
Arguments:
- panel: bfloat16 [8192, 4096], P('prow', 'pcol'), may hold values from -0.09375 to 0.09375
- anc_inverse: bfloat16 [8192, 8192], P('prow', 'pcol'), may hold values from -6 to 6
- diag_inverse: bfloat16 [4096, 4096], P('prow', 'pcol'), may hold values from -6 to 6
- block_counts: int32 [16], replicated, may hold values from 0 to 4, as said below
Outputs:
- off_diag: bfloat16 [8192, 4096], P('prow', 'pcol')
- diag_block: float32 [4096, 4096], P('prow', 'pcol')
Inputs may be any that keep to these rules, and one draw needn't show every extreme that they name: `block_counts`: they add up to exactly 32, and some grid row owns 4 blocks.
All inputs are finite; a program needn't handle non-finite values.
Results may differ from a plain program's by a relative error of at most 0.002.
Values may be sent and summed in bfloat16 or wider, within the bound.
No kernel may reach another device: no remote copies, remote signals or barrier semaphores. Data moves between devices by JAX's collectives and lax.ppermute only.
A program may use at most 128 MiB of HBM per device.

v0:
```python
import jax
import jax.numpy as jnp
from jax import lax
from jax.sharding import PartitionSpec as P

BLK = 128


def per_device(panel, anc_inverse, diag_inverse, block_counts):
    grid_row = lax.axis_index("prow")
    slot_rows = panel.shape[0]
    own_count = block_counts[grid_row]
    in_use = jnp.arange(slot_rows) // BLK < own_count
    masked = jnp.where(in_use[:, None], panel, jnp.zeros_like(panel))
    whole_rows = lax.all_gather(masked, "pcol", axis=1, tiled=True)
    all_panel = lax.all_gather(masked, "prow", axis=0, tiled=True)
    all_inverse = lax.all_gather(anc_inverse, "pcol", axis=1, tiled=True)
    product = jnp.dot(all_inverse, all_panel, preferred_element_type=jnp.float32)
    off_diag = jnp.where(in_use[:, None], -product, 0.0).astype(jnp.bfloat16)
    summed = lax.psum_scatter(
        lax.dot_general(
            whole_rows, off_diag, (((0,), (0,)), ((), ())), preferred_element_type=jnp.float32
        ),
        "prow",
        scatter_dimension=0,
        tiled=True,
    )
    diag_block = diag_inverse.astype(jnp.float32) - summed
    return (off_diag, diag_block)


def solution(mesh):
    return jax.shard_map(
        per_device,
        mesh=mesh,
        in_specs=(P("prow", "pcol"), P("prow", "pcol"), P("prow", "pcol"), P()),
        out_specs=(P("prow", "pcol"), P("prow", "pcol")),
        check_vma=False,
    )
```

profile of v0, /device:TPU:0, one launch (start us, length us, event | category | flops | bytes accessed | tf_op | source)
XLA Modules:
  0.0 703.6 jit_solution(9929988382303146813)
XLA Ops:
  7.2 0.0 copy-start.2
  7.2 0.0 copy-start
  7.2 0.0 all-gather.6.cloned.1.call-start
  7.2 0.7 all-gather.6.cloned.1.call-update
  7.9 0.0 all-gather.4.cloned.1.call-start
  8.0 0.0 copy-done.2
  8.0 0.6 dynamic_slice.3
  8.6 0.7 fusion
  9.2 0.0 copy-done
  9.2 1.5 broadcast_select_fusion
  10.8 0.0 all-gather.4.cloned.1.call-update
  10.8 0.0 all-gather.8.cloned.1.call-start
  10.8 0.7 all-gather.8.cloned.1.call-update
  11.5 0.0 reduce-scatter.2.cloned.1.call-start
  11.6 104.7 %all-gather.6.cloned.1.call-done = bf16[512,8192]{1,0:T(8,128)(2,1)} async-done(((bf16[512,4096]{1,0:T(8,128)(2,1)}), bf16[512,8192]{1,0:T(8,128)(2,1)}) %all-gather.6.cloned.1.call-update) | async-done | bytes 8388624 | tf_op jit(solution)/shard_map/all_gather | solution.py:17
  116.3 170.2 %all-gather.4.cloned.1.call-done = bf16[8192,2048]{1,0:T(8,128)(2,1)} async-done(((bf16[512,2048]{1,0:T(8,128)(2,1)}), bf16[8192,2048]{1,0:T(8,128)(2,1)}) %all-gather.4.cloned.1.call-update) | async-done | bytes 33554448 | tf_op jit(solution)/shard_map/all_gather | solution.py:16
  286.5 24.0 %select_convert_fusion = bf16[2048,512]{1,0:T(8,128)(2,1)S(1)} fusion(bf16[8192,2048]{1,0:T(8,128)(2,1)} %all-gather.4.cloned.1.call-done, bf16[512,8192]{1,0:T(8,128)(2,1)} %all-gather.6.cloned.1.call-done, pred[512]{0:T(512)(128)(4,1)S(1)} %fusion), kind=kOutput, calls=%fused_computation | convolution fusion | flops 17183014912 | bytes 44040704 | tf_op jit(solution)/shard_map/dot_general | solution.py:18
  310.5 34.8 %all-gather.8.cloned.1.call-done = bf16[512,4096]{1,0:T(8,128)(2,1)} async-done(((bf16[512,2048]{1,0:T(8,128)(2,1)}), bf16[512,4096]{1,0:T(8,128)(2,1)}) %all-gather.8.cloned.1.call-update) | async-done | bytes 4194320 | tf_op jit(solution)/shard_map/all_gather | solution.py:15
  345.4 17.6 %fusion.4 = f32[4096,2048]{1,0:T(8,128)} fusion(bf16[512,4096]{1,0:T(8,128)(2,1)} %all-gather.8.cloned.1.call-done, bf16[2048,512]{1,0:T(8,128)(2,1)S(1)} %select_convert_fusion), kind=kOutput, calls=%fused_computation.11 | convolution fusion | flops 8589934592 | bytes 39845888 | tf_op jit(solution)/shard_map/dot_general | solution.py:21
  363.0 0.0 reduce-scatter.2.cloned.1.call-update
  363.0 0.0 copy-start.1
  363.0 2.4 copy.6
  365.4 328.4 %reduce-scatter.2.cloned.1.call-done = f32[256,2048]{1,0:T(8,128)} async-done(((f32[4096,2048]{1,0:T(8,128)}), f32[256,2048]{1,0:T(8,128)}) %reduce-scatter.2.cloned.1.call-update) | async-done | bytes 2097168 | tf_op jit(solution)/shard_map/reduce_scatter | solution.py:20
  693.8 0.0 copy-done.1
  693.8 3.3 convert_subtract_fusion
Async XLA Ops:
  7.2 0.8 copy-start.2
  7.2 2.1 copy-start
  7.2 109.1 %all-gather.6.cloned.1.call-start = ((), (), s32[]{:S(2)}) async-start(), calls=%async_computation.2 | async-start | bytes 12582912 | tf_op jit(solution)/shard_map/all_gather | solution.py:17
  7.9 278.6 %all-gather.4.cloned.1.call-start = ((), (), s32[]{:S(2)}) async-start(), calls=%async_computation.1 | async-start | bytes 35651584 | tf_op jit(solution)/shard_map/all_gather | solution.py:16
  10.8 334.6 %all-gather.8.cloned.1.call-start = ((), (), s32[]{:S(2)}) async-start(), calls=%async_computation.3 | async-start | bytes 6291456 | tf_op jit(solution)/shard_map/all_gather | solution.py:15
  11.5 682.3 %reduce-scatter.2.cloned.1.call-start = ((), (), s32[]{:S(2)}) async-start(), calls=%async_computation.4 | async-start | bytes 35651584 | tf_op jit(solution)/shard_map/reduce_scatter | solution.py:20
  363.0 330.8 %copy-start.1 = (bf16[256,2048]{1,0:T(8,128)(2,1)S(1)}, bf16[256,2048]{1,0:T(8,128)(2,1)}, u32[]{:S(2)}) copy-start(bf16[256,2048]{1,0:T(8,128)(2,1)} %param.6) | copy-start | bytes 3145732
Sparse Core Ops, SparseCore 0:
  9.5 106.6 all-gather.5
  118.4 168.0 all-gather.3
  288.6 56.6 all-gather.7
  363.2 330.5 reduce-scatter.1
where the time goes:
time: 704 us
  waiting for transfers between devices  640 us (91%)
  matrix products  41.6 us (6%)
  between operations  13.8 us (2%)
    reduce_scatter x1, waiting for transfers between devices, per_device(): lax.psum_scatter(lax.dot_general(whole_rows, off_diag, (((0,), (0,)), (()...  328 us
    all_gather x1, waiting for transfers between devices, per_device(): all_panel = lax.all_gather(masked, 'prow', axis=0, tiled=True)  170 us
    all_gather x1, waiting for transfers between devices, per_device(): all_inverse = lax.all_gather(anc_inverse, 'pcol', axis=1, tiled=True)  105 us
    all_gather x1, waiting for transfers between devices, per_device(): whole_rows = lax.all_gather(masked, 'pcol', axis=1, tiled=True)  34.8 us
    dot_general x1, matrix products, per_device(): jnp.dot(all_inverse, all_panel, preferred_element_type=jnp.float32)  24 us
    dot_general x1, matrix products, per_device(): lax.dot_general(whole_rows, off_diag, (((0,), (0,)), ((), ())), preferred...  17.6 us
  transfers between devices with their start and end apart: 4, of which 4 were waited for; matrix products, arithmetic and copies ran while one was open for 4% of the time, Pallas kernels for 0%

commit v1 on v0

--- a/solution.py
+++ b/solution.py
@@ -13,7 +13,12 @@
     in_use = jnp.arange(slot_rows) // BLK < own_count
     masked = jnp.where(in_use[:, None], panel, jnp.zeros_like(panel))
     whole_rows = lax.all_gather(masked, "pcol", axis=1, tiled=True)
-    all_panel = lax.all_gather(masked, "prow", axis=0, tiled=True)
+    ring = [masked]
+    for hop in range(15):
+        ring.append(lax.ppermute(ring[-1], "prow", [(dev, (dev + 1) % 16) for dev in range(16)]))
+    all_panel = jnp.roll(
+        jnp.concatenate(ring[::-1], axis=0), (lax.axis_index("prow") + 1) * ring[0].shape[0], axis=0
+    )
     all_inverse = lax.all_gather(anc_inverse, "pcol", axis=1, tiled=True)
     product = jnp.dot(all_inverse, all_panel, preferred_element_type=jnp.float32)
     off_diag = jnp.where(in_use[:, None], -product, 0.0).astype(jnp.bfloat16)

time: 704 us -> 913 us (1.30)
  waiting for transfers between devices: 640 us -> 750 us
  local copies, waits for them, and re-layouts: 2.98 us -> 95.6 us
    ppermute x0 -> x15, waiting for transfers between devices: none -> 424 us  [per_device(): lax.ppermute(ring[-1], 'prow', [(dev, (dev + 1) % 16) for dev in range(16)])]
    all_gather x1 -> x0, waiting for transfers between devices: 170 us -> none  [per_device(): all_panel = lax.all_gather(masked, 'prow', axis=0, tiled=True)]
    all_gather x1, waiting for transfers between devices: 105 us -> 0.01 us  [per_device(): all_inverse = lax.all_gather(anc_inverse, 'pcol', axis=1, tiled=True)]
    unnamed x7 -> x79, local copies, waits for them, and re-layouts: 2.39 us -> 94.2 us
    all_gather x1, waiting for transfers between devices: 34.8 us -> 0.02 us  [per_device(): whole_rows = lax.all_gather(masked, 'pcol', axis=1, tiled=True)]
  transfers between devices with their start and end apart: 4 -> 18, of which waited for: 4 -> 16; matrix products, arithmetic and copies ran while one was open for 4% -> 12% of each run, Pallas kernels for 0% -> 0%
where the time goes in v1:
time: 913 us; the launch traced here: 912 us
  waiting for transfers between devices  750 us (82%)
  local copies, waits for them, and re-layouts  95.6 us (10%)
  matrix products  41.6 us (5%)
  between operations  13.9 us (2%)
  other arithmetic  10.5 us (1%)
    ppermute x15, waiting for transfers between devices, per_device(): lax.ppermute(ring[-1], 'prow', [(dev, (dev + 1) % 16) for dev in range(16)])  424 us
    reduce_scatter x1, waiting for transfers between devices, per_device(): lax.psum_scatter(lax.dot_general(whole_rows, off_diag, (((0,), (0,)), (()...  326 us
    unnamed x79, local copies, waits for them, and re-layouts  94.2 us
    dot_general x1, matrix products, per_device(): jnp.dot(all_inverse, all_panel, preferred_element_type=jnp.float32)  24 us
  transfers between devices with their start and end apart: 18, of which 16 were waited for; matrix products, arithmetic and copies ran while one was open for 12% of the time, Pallas kernels for 0%

profile of v1, /device:TPU:0, one launch (start us, length us, event | category | flops | bytes accessed | tf_op | source)
XLA Modules:
  0.0 912.3 jit_solution(17857974493092935983)
XLA Ops:
  9.3 3.1 broadcast_select_fusion
  12.9 28.9 %collective-permute-done = bf16[512,2048]{1,0:T(8,128)(2,1)S(1)} collective-permute-done((bf16[512,2048]{1,0:T(8,128)(2,1)}, bf16[512,2048]{1,0:T(8,128)(2,1)S(1)}, u32[]{:S(2)}, u32[]{:S(2)}) %collective-permute-start) | collective-permute-done | bytes 2097184 | tf_op jit(solution)/shard_map/ppermute | solution.py:18
  43.1 28.2 %collective-permute-done.1 = bf16[512,2048]{1,0:T(8,128)(2,1)S(1)} collective-permute-done((bf16[512,2048]{1,0:T(8,128)(2,1)S(1)}, bf16[512,2048]{1,0:T(8,128)(2,1)S(1)}, u32[]{:S(2)}, u32[]{:S(2)}) %collective-permute-start.1) | collective-permute-done | bytes 2097184 | tf_op jit(solution)/shard_map/ppermute | solution.py:18
  72.6 28.2 %collective-permute-done.2 = bf16[512,2048]{1,0:T(8,128)(2,1)S(1)} collective-permute-done((bf16[512,2048]{1,0:T(8,128)(2,1)S(1)}, bf16[512,2048]{1,0:T(8,128)(2,1)S(1)}, u32[]{:S(2)}, u32[]{:S(2)}) %collective-permute-start.2) | collective-permute-done | bytes 2097184 | tf_op jit(solution)/shard_map/ppermute | solution.py:18
  102.1 28.2 %collective-permute-done.3 = bf16[512,2048]{1,0:T(8,128)(2,1)S(1)} collective-permute-done((bf16[512,2048]{1,0:T(8,128)(2,1)S(1)}, bf16[512,2048]{1,0:T(8,128)(2,1)S(1)}, u32[]{:S(2)}, u32[]{:S(2)}) %collective-permute-start.3) | collective-permute-done | bytes 2097184 | tf_op jit(solution)/shard_map/ppermute | solution.py:18
  131.6 28.2 %collective-permute-done.4 = bf16[512,2048]{1,0:T(8,128)(2,1)S(1)} collective-permute-done((bf16[512,2048]{1,0:T(8,128)(2,1)S(1)}, bf16[512,2048]{1,0:T(8,128)(2,1)S(1)}, u32[]{:S(2)}, u32[]{:S(2)}) %collective-permute-start.4) | collective-permute-done | bytes 2097184 | tf_op jit(solution)/shard_map/ppermute | solution.py:18
  161.1 28.2 %collective-permute-done.5 = bf16[512,2048]{1,0:T(8,128)(2,1)S(1)} collective-permute-done((bf16[512,2048]{1,0:T(8,128)(2,1)S(1)}, bf16[512,2048]{1,0:T(8,128)(2,1)S(1)}, u32[]{:S(2)}, u32[]{:S(2)}) %collective-permute-start.5) | collective-permute-done | bytes 2097184 | tf_op jit(solution)/shard_map/ppermute | solution.py:18
  190.6 28.2 %collective-permute-done.6 = bf16[512,2048]{1,0:T(8,128)(2,1)S(1)} collective-permute-done((bf16[512,2048]{1,0:T(8,128)(2,1)S(1)}, bf16[512,2048]{1,0:T(8,128)(2,1)S(1)}, u32[]{:S(2)}, u32[]{:S(2)}) %collective-permute-start.6) | collective-permute-done | bytes 2097184 | tf_op jit(solution)/shard_map/ppermute | solution.py:18
  220.1 28.2 %collective-permute-done.7 = bf16[512,2048]{1,0:T(8,128)(2,1)S(1)} collective-permute-done((bf16[512,2048]{1,0:T(8,128)(2,1)S(1)}, bf16[512,2048]{1,0:T(8,128)(2,1)S(1)}, u32[]{:S(2)}, u32[]{:S(2)}) %collective-permute-start.7) | collective-permute-done | bytes 2097184 | tf_op jit(solution)/shard_map/ppermute | solution.py:18
  249.7 28.2 %collective-permute-done.8 = bf16[512,2048]{1,0:T(8,128)(2,1)S(1)} collective-permute-done((bf16[512,2048]{1,0:T(8,128)(2,1)S(1)}, bf16[512,2048]{1,0:T(8,128)(2,1)S(1)}, u32[]{:S(2)}, u32[]{:S(2)}) %collective-permute-start.8) | collective-permute-done | bytes 2097184 | tf_op jit(solution)/shard_map/ppermute | solution.py:18
  279.2 28.3 %collective-permute-done.9 = bf16[512,2048]{1,0:T(8,128)(2,1)} collective-permute-done((bf16[512,2048]{1,0:T(8,128)(2,1)S(1)}, bf16[512,2048]{1,0:T(8,128)(2,1)}, u32[]{:S(2)}, u32[]{:S(2)}) %collective-permute-start.9) | collective-permute-done | bytes 2097184 | tf_op jit(solution)/shard_map/ppermute | solution.py:18
  307.5 28.4 %collective-permute-done.10 = bf16[512,2048]{1,0:T(8,128)(2,1)} collective-permute-done((bf16[512,2048]{1,0:T(8,128)(2,1)}, bf16[512,2048]{1,0:T(8,128)(2,1)}, u32[]{:S(2)}, u32[]{:S(2)}) %collective-permute-start.10) | collective-permute-done | bytes 2097184 | tf_op jit(solution)/shard_map/ppermute | solution.py:18
  335.9 28.4 %collective-permute-done.11 = bf16[512,2048]{1,0:T(8,128)(2,1)S(1)} collective-permute-done((bf16[512,2048]{1,0:T(8,128)(2,1)}, bf16[512,2048]{1,0:T(8,128)(2,1)S(1)}, u32[]{:S(2)}, u32[]{:S(2)}) %collective-permute-start.11) | collective-permute-done | bytes 2097184 | tf_op jit(solution)/shard_map/ppermute | solution.py:18
  365.6 28.2 %collective-permute-done.12 = bf16[512,2048]{1,0:T(8,128)(2,1)S(1)} collective-permute-done((bf16[512,2048]{1,0:T(8,128)(2,1)S(1)}, bf16[512,2048]{1,0:T(8,128)(2,1)S(1)}, u32[]{:S(2)}, u32[]{:S(2)}) %collective-permute-start.12) | collective-permute-done | bytes 2097184 | tf_op jit(solution)/shard_map/ppermute | solution.py:18
  395.1 28.3 %collective-permute-done.13 = bf16[512,2048]{1,0:T(8,128)(2,1)} collective-permute-done((bf16[512,2048]{1,0:T(8,128)(2,1)S(1)}, bf16[512,2048]{1,0:T(8,128)(2,1)}, u32[]{:S(2)}, u32[]{:S(2)}) %collective-permute-start.13) | collective-permute-done | bytes 2097184 | tf_op jit(solution)/shard_map/ppermute | solution.py:18
  423.5 28.3 %collective-permute-done.14 = bf16[512,2048]{1,0:T(8,128)(2,1)} collective-permute-done((bf16[512,2048]{1,0:T(8,128)(2,1)}, bf16[512,2048]{1,0:T(8,128)(2,1)}, u32[]{:S(2)}, u32[]{:S(2)}) %collective-permute-start.14) | collective-permute-done | bytes 2097184 | tf_op jit(solution)/shard_map/ppermute | solution.py:18
  451.8 3.2 constant_dynamic-update-slice_fusion.31
  455.0 3.2 constant_dynamic-update-slice_fusion.30
  458.2 3.2 constant_dynamic-update-slice_fusion.29
  461.4 3.2 constant_dynamic-update-slice_fusion.28
  464.6 3.2 constant_dynamic-update-slice_fusion.27
  467.8 3.2 constant_dynamic-update-slice_fusion.26
  471.0 3.1 constant_dynamic-update-slice_fusion.25
  474.1 3.1 constant_dynamic-update-slice_fusion.24
  477.3 3.2 constant_dynamic-update-slice_fusion.23
  480.5 3.2 constant_dynamic-update-slice_fusion.22
  483.6 3.2 constant_dynamic-update-slice_fusion.21
  486.8 3.2 constant_dynamic-update-slice_fusion.20
  490.1 3.2 constant_dynamic-update-slice_fusion.19
  493.3 3.2 constant_dynamic-update-slice_fusion.18
  496.5 3.1 constant_dynamic-update-slice_fusion.17
  499.6 1.7 constant_dynamic-update-slice_fusion.16
  501.4 3.2 constant_dynamic-update-slice_fusion.15
  504.6 3.2 constant_dynamic-update-slice_fusion.14
  509.2 1.5 constant_dynamic-update-slice_fusion.12
  510.7 3.2 constant_dynamic-update-slice_fusion.11
  513.9 3.2 constant_dynamic-update-slice_fusion.10
  517.1 1.5 constant_dynamic-update-slice_fusion.9
  518.6 1.5 constant_dynamic-update-slice_fusion.8
  524.6 1.5 constant_dynamic-update-slice_fusion.4
  527.6 1.5 constant_dynamic-update-slice_fusion.2
  529.1 1.5 constant_dynamic-update-slice_fusion.1
  530.6 1.7 constant_dynamic-update-slice_fusion
  532.3 24.0 %select_convert_fusion = bf16[2048,512]{1,0:T(8,128)(2,1)S(1)} fusion(bf16[512,8192]{1,0:T(8,128)(2,1)} %all-gather.3.cloned.1.call-done, bf16[16384,2048]{1,0:T(8,128)(2,1)} %constant_dynamic-update-slice_fusion, s32[]{:T(128)S(6)} %select_n.38, pred[512]{0:T(512)(128)(4,1)S(1)} %fusion.4), kind=kOutput, calls=%fused_computation.2 | convolution fusion | flops 17183014912 | bytes 44040708 | tf_op jit(solution)/shard_map/dot_general | solution.py:23
  556.4 17.6 %fusion.9 = f32[4096,2048]{1,0:T(8,128)} fusion(bf16[512,4096]{1,0:T(8,128)(2,1)} %all-gather.5.cloned.1.call-done, bf16[2048,512]{1,0:T(8,128)(2,1)S(1)} %select_convert_fusion), kind=kOutput, calls=%fused_computation.46 | convolution fusion | flops 8589934592 | bytes 39845888 | tf_op jit(solution)/shard_map/dot_general | solution.py:26
  574.0 2.4 copy.6
  576.4 326.1 %reduce-scatter.2.cloned.1.call-done = f32[256,2048]{1,0:T(8,128)} async-done(((f32[4096,2048]{1,0:T(8,128)}), f32[256,2048]{1,0:T(8,128)}) %reduce-scatter.2.cloned.1.call-update) | async-done | bytes 2097168 | tf_op jit(solution)/shard_map/reduce_scatter | solution.py:25
  902.5 3.3 convert_subtract_fusion
  (78 shorter events, 25.0 us)
Async XLA Ops:
  7.2 492.5 %copy-start = (bf16[512,2048]{1,0:T(8,128)(2,1)S(1)}, bf16[512,2048]{1,0:T(8,128)(2,1)}, u32[]{:S(2)}) copy-start(bf16[512,2048]{1,0:T(8,128)(2,1)} %param.4) | copy-start | bytes 6291460
  7.2 525.2 %all-gather.3.cloned.1.call-start = ((), (), s32[]{:S(2)}) async-start(), calls=%async_computation.1 | async-start | bytes 12582912 | tf_op jit(solution)/shard_map/all_gather | solution.py:22
  12.4 29.4 %collective-permute-start = (bf16[512,2048]{1,0:T(8,128)(2,1)}, bf16[512,2048]{1,0:T(8,128)(2,1)S(1)}, u32[]{:S(2)}, u32[]{:S(2)}) collective-permute-start(bf16[512,2048]{1,0:T(8,128)(2,1)} %broadcast_select_fusion), channel_id=1, source_target_pairs={{0,2},{2,4},{4,6},{6,8},{8,10},{10,12},{12,14},{14,16},{16,18},{18... | collective-permute-start | bytes 6291464 | tf_op jit(solution)/shard_map/ppermute | solution.py:18
  41.8 1.3 copy-start.1
  43.1 28.2 %collective-permute-start.1 = (bf16[512,2048]{1,0:T(8,128)(2,1)S(1)}, bf16[512,2048]{1,0:T(8,128)(2,1)S(1)}, u32[]{:S(2)}, u32[]{:S(2)}) collective-permute-start(bf16[512,2048]{1,0:T(8,128)(2,1)S(1)} %collective-permute-done), channel_id=1, source_target_pairs={{0,2},{2,4},{4,6},{6,8},{8,10},{10,12},{12,14},{14,16},{16,18},{18... | collective-permute-start | bytes 6291464 | tf_op jit(solution)/shard_map/ppermute | solution.py:18
  71.2 1.3 copy-start.3
  72.6 28.2 %collective-permute-start.2 = (bf16[512,2048]{1,0:T(8,128)(2,1)S(1)}, bf16[512,2048]{1,0:T(8,128)(2,1)S(1)}, u32[]{:S(2)}, u32[]{:S(2)}) collective-permute-start(bf16[512,2048]{1,0:T(8,128)(2,1)S(1)} %collective-permute-done.1), channel_id=1, source_target_pairs={{0,2},{2,4},{4,6},{6,8},{8,10},{10,12},{12,14},{14,16},{16,18},{18... | collective-permute-start | bytes 6291464 | tf_op jit(solution)/shard_map/ppermute | solution.py:18
  100.7 1.4 copy-start.5
  102.1 28.2 %collective-permute-start.3 = (bf16[512,2048]{1,0:T(8,128)(2,1)S(1)}, bf16[512,2048]{1,0:T(8,128)(2,1)S(1)}, u32[]{:S(2)}, u32[]{:S(2)}) collective-permute-start(bf16[512,2048]{1,0:T(8,128)(2,1)S(1)} %collective-permute-done.2), channel_id=1, source_target_pairs={{0,2},{2,4},{4,6},{6,8},{8,10},{10,12},{12,14},{14,16},{16,18},{18... | collective-permute-start | bytes 6291464 | tf_op jit(solution)/shard_map/ppermute | solution.py:18
  130.3 1.4 copy-start.7
  131.6 28.2 %collective-permute-start.4 = (bf16[512,2048]{1,0:T(8,128)(2,1)S(1)}, bf16[512,2048]{1,0:T(8,128)(2,1)S(1)}, u32[]{:S(2)}, u32[]{:S(2)}) collective-permute-start(bf16[512,2048]{1,0:T(8,128)(2,1)S(1)} %collective-permute-done.3), channel_id=1, source_target_pairs={{0,2},{2,4},{4,6},{6,8},{8,10},{10,12},{12,14},{14,16},{16,18},{18... | collective-permute-start | bytes 6291464 | tf_op jit(solution)/shard_map/ppermute | solution.py:18
  159.8 1.3 copy-start.9
  161.1 28.2 %collective-permute-start.5 = (bf16[512,2048]{1,0:T(8,128)(2,1)S(1)}, bf16[512,2048]{1,0:T(8,128)(2,1)S(1)}, u32[]{:S(2)}, u32[]{:S(2)}) collective-permute-start(bf16[512,2048]{1,0:T(8,128)(2,1)S(1)} %collective-permute-done.4), channel_id=1, source_target_pairs={{0,2},{2,4},{4,6},{6,8},{8,10},{10,12},{12,14},{14,16},{16,18},{18... | collective-permute-start | bytes 6291464 | tf_op jit(solution)/shard_map/ppermute | solution.py:18
  189.3 1.3 copy-start.11
  190.6 28.2 %collective-permute-start.6 = (bf16[512,2048]{1,0:T(8,128)(2,1)S(1)}, bf16[512,2048]{1,0:T(8,128)(2,1)S(1)}, u32[]{:S(2)}, u32[]{:S(2)}) collective-permute-start(bf16[512,2048]{1,0:T(8,128)(2,1)S(1)} %collective-permute-done.5), channel_id=1, source_target_pairs={{0,2},{2,4},{4,6},{6,8},{8,10},{10,12},{12,14},{14,16},{16,18},{18... | collective-permute-start | bytes 6291464 | tf_op jit(solution)/shard_map/ppermute | solution.py:18
  218.8 1.3 copy-start.13
  220.1 28.2 %collective-permute-start.7 = (bf16[512,2048]{1,0:T(8,128)(2,1)S(1)}, bf16[512,2048]{1,0:T(8,128)(2,1)S(1)}, u32[]{:S(2)}, u32[]{:S(2)}) collective-permute-start(bf16[512,2048]{1,0:T(8,128)(2,1)S(1)} %collective-permute-done.6), channel_id=1, source_target_pairs={{0,2},{2,4},{4,6},{6,8},{8,10},{10,12},{12,14},{14,16},{16,18},{18... | collective-permute-start | bytes 6291464 | tf_op jit(solution)/shard_map/ppermute | solution.py:18
  248.2 1.4 copy-start.15
  249.7 28.2 %collective-permute-start.8 = (bf16[512,2048]{1,0:T(8,128)(2,1)S(1)}, bf16[512,2048]{1,0:T(8,128)(2,1)S(1)}, u32[]{:S(2)}, u32[]{:S(2)}) collective-permute-start(bf16[512,2048]{1,0:T(8,128)(2,1)S(1)} %collective-permute-done.7), channel_id=1, source_target_pairs={{0,2},{2,4},{4,6},{6,8},{8,10},{10,12},{12,14},{14,16},{16,18},{18... | collective-permute-start | bytes 6291464 | tf_op jit(solution)/shard_map/ppermute | solution.py:18
  277.8 1.3 copy-start.17
  279.2 28.3 %collective-permute-start.9 = (bf16[512,2048]{1,0:T(8,128)(2,1)S(1)}, bf16[512,2048]{1,0:T(8,128)(2,1)}, u32[]{:S(2)}, u32[]{:S(2)}) collective-permute-start(bf16[512,2048]{1,0:T(8,128)(2,1)S(1)} %collective-permute-done.8), channel_id=1, source_target_pairs={{0,2},{2,4},{4,6},{6,8},{8,10},{10,12},{12,14},{14,16},{16,18},{18... | collective-permute-start | bytes 6291464 | tf_op jit(solution)/shard_map/ppermute | solution.py:18
  307.4 28.5 %collective-permute-start.10 = (bf16[512,2048]{1,0:T(8,128)(2,1)}, bf16[512,2048]{1,0:T(8,128)(2,1)}, u32[]{:S(2)}, u32[]{:S(2)}) collective-permute-start(bf16[512,2048]{1,0:T(8,128)(2,1)} %collective-permute-done.9), channel_id=1, source_target_pairs={{0,2},{2,4},{4,6},{6,8},{8,10},{10,12},{12,14},{14,16},{16,18},{18... | collective-permute-start | bytes 6291464 | tf_op jit(solution)/shard_map/ppermute | solution.py:18
  307.4 248.9 %all-gather.5.cloned.1.call-start = ((), (), s32[]{:S(2)}) async-start(), calls=%async_computation.2 | async-start | bytes 6291456 | tf_op jit(solution)/shard_map/all_gather | solution.py:15
  335.9 28.4 %collective-permute-start.11 = (bf16[512,2048]{1,0:T(8,128)(2,1)}, bf16[512,2048]{1,0:T(8,128)(2,1)S(1)}, u32[]{:S(2)}, u32[]{:S(2)}) collective-permute-start(bf16[512,2048]{1,0:T(8,128)(2,1)} %collective-permute-done.10), channel_id=1, source_target_pairs={{0,2},{2,4},{4,6},{6,8},{8,10},{10,12},{12,14},{14,16},{16,18},{18... | collective-permute-start | bytes 6291464 | tf_op jit(solution)/shard_map/ppermute | solution.py:18
  364.3 1.3 copy-start.19
  365.6 28.2 %collective-permute-start.12 = (bf16[512,2048]{1,0:T(8,128)(2,1)S(1)}, bf16[512,2048]{1,0:T(8,128)(2,1)S(1)}, u32[]{:S(2)}, u32[]{:S(2)}) collective-permute-start(bf16[512,2048]{1,0:T(8,128)(2,1)S(1)} %collective-permute-done.11), channel_id=1, source_target_pairs={{0,2},{2,4},{4,6},{6,8},{8,10},{10,12},{12,14},{14,16},{16,18},{18... | collective-permute-start | bytes 6291464 | tf_op jit(solution)/shard_map/ppermute | solution.py:18
  393.7 1.3 copy-start.21
  395.1 28.3 %collective-permute-start.13 = (bf16[512,2048]{1,0:T(8,128)(2,1)S(1)}, bf16[512,2048]{1,0:T(8,128)(2,1)}, u32[]{:S(2)}, u32[]{:S(2)}) collective-permute-start(bf16[512,2048]{1,0:T(8,128)(2,1)S(1)} %collective-permute-done.12), channel_id=1, source_target_pairs={{0,2},{2,4},{4,6},{6,8},{8,10},{10,12},{12,14},{14,16},{16,18},{18... | collective-permute-start | bytes 6291464 | tf_op jit(solution)/shard_map/ppermute | solution.py:18
  423.3 28.5 %collective-permute-start.14 = (bf16[512,2048]{1,0:T(8,128)(2,1)}, bf16[512,2048]{1,0:T(8,128)(2,1)}, u32[]{:S(2)}, u32[]{:S(2)}) collective-permute-start(bf16[512,2048]{1,0:T(8,128)(2,1)} %collective-permute-done.13), channel_id=1, source_target_pairs={{0,2},{2,4},{4,6},{6,8},{8,10},{10,12},{12,14},{14,16},{16,18},{18... | collective-permute-start | bytes 6291464 | tf_op jit(solution)/shard_map/ppermute | solution.py:18
  423.3 479.1 %reduce-scatter.2.cloned.1.call-start = ((), (), s32[]{:S(2)}) async-start(), calls=%async_computation.3 | async-start | bytes 35651584 | tf_op jit(solution)/shard_map/reduce_scatter | solution.py:25
  423.4 84.3 %copy-start.22 = (bf16[512,2048]{1,0:T(8,128)(2,1)S(1)}, bf16[512,2048]{1,0:T(8,128)(2,1)}, u32[]{:S(2)}) copy-start(bf16[512,2048]{1,0:T(8,128)(2,1)} %copy-done.21) | copy-start | bytes 6291460
  423.4 85.8 %copy-start.20 = (bf16[512,2048]{1,0:T(8,128)(2,1)S(1)}, bf16[512,2048]{1,0:T(8,128)(2,1)}, u32[]{:S(2)}) copy-start(bf16[512,2048]{1,0:T(8,128)(2,1)} %copy-done.19) | copy-start | bytes 6291460
  423.4 93.7 %copy-start.18 = (bf16[512,2048]{1,0:T(8,128)(2,1)S(1)}, bf16[512,2048]{1,0:T(8,128)(2,1)}, u32[]{:S(2)}) copy-start(bf16[512,2048]{1,0:T(8,128)(2,1)} %copy-done.17) | copy-start | bytes 6291460
  423.4 95.2 %copy-start.16 = (bf16[512,2048]{1,0:T(8,128)(2,1)S(1)}, bf16[512,2048]{1,0:T(8,128)(2,1)}, u32[]{:S(2)}) copy-start(bf16[512,2048]{1,0:T(8,128)(2,1)} %copy-done.15) | copy-start | bytes 6291460
  423.5 96.7 %copy-start.14 = (bf16[512,2048]{1,0:T(8,128)(2,1)S(1)}, bf16[512,2048]{1,0:T(8,128)(2,1)}, u32[]{:S(2)}) copy-start(bf16[512,2048]{1,0:T(8,128)(2,1)} %copy-done.13) | copy-start | bytes 6291460
  423.5 98.1 %copy-start.12 = (bf16[512,2048]{1,0:T(8,128)(2,1)S(1)}, bf16[512,2048]{1,0:T(8,128)(2,1)}, u32[]{:S(2)}) copy-start(bf16[512,2048]{1,0:T(8,128)(2,1)} %copy-done.11) | copy-start | bytes 6291460
  423.5 99.6 %copy-start.10 = (bf16[512,2048]{1,0:T(8,128)(2,1)S(1)}, bf16[512,2048]{1,0:T(8,128)(2,1)}, u32[]{:S(2)}) copy-start(bf16[512,2048]{1,0:T(8,128)(2,1)} %copy-done.9) | copy-start | bytes 6291460
  423.5 101.1 %copy-start.8 = (bf16[512,2048]{1,0:T(8,128)(2,1)S(1)}, bf16[512,2048]{1,0:T(8,128)(2,1)}, u32[]{:S(2)}) copy-start(bf16[512,2048]{1,0:T(8,128)(2,1)} %copy-done.7) | copy-start | bytes 6291460
  423.5 102.6 %copy-start.6 = (bf16[512,2048]{1,0:T(8,128)(2,1)S(1)}, bf16[512,2048]{1,0:T(8,128)(2,1)}, u32[]{:S(2)}) copy-start(bf16[512,2048]{1,0:T(8,128)(2,1)} %copy-done.5) | copy-start | bytes 6291460
  423.5 104.1 %copy-start.4 = (bf16[512,2048]{1,0:T(8,128)(2,1)S(1)}, bf16[512,2048]{1,0:T(8,128)(2,1)}, u32[]{:S(2)}) copy-start(bf16[512,2048]{1,0:T(8,128)(2,1)} %copy-done.3) | copy-start | bytes 6291460
  423.5 105.6 %copy-start.2 = (bf16[512,2048]{1,0:T(8,128)(2,1)S(1)}, bf16[512,2048]{1,0:T(8,128)(2,1)}, u32[]{:S(2)}) copy-start(bf16[512,2048]{1,0:T(8,128)(2,1)} %copy-done.1) | copy-start | bytes 6291460
  556.4 346.1 %copy-start.23 = (bf16[256,2048]{1,0:T(8,128)(2,1)S(1)}, bf16[256,2048]{1,0:T(8,128)(2,1)}, u32[]{:S(2)}) copy-start(bf16[256,2048]{1,0:T(8,128)(2,1)} %param.6) | copy-start | bytes 3145732
Sparse Core Ops, SparseCore 0:
  307.6 105.6 all-gather.2
  423.5 58.3 all-gather.4
  574.1 328.3 reduce-scatter.1
